TPU v7x, 256 devices: a whole 4x4x8 slice. The times are simulated.
256 devices in a mesh: group: 8 (over x, core), expert: 32 (over y, z).
Axes of the slice: x: 4, y: 4, z: 8, core: 2. Of those that a mesh axis runs over, the one named last changes fastest.
Arguments:
- resid: bfloat16 [32768, 2048], P(('group', 'expert')), may hold values from -6 to 6
- queries: bfloat16 [32768, 2048], P(('group', 'expert')), may hold values from -48 to 48
- span_kv: bfloat16 [2, 32768, 2048], P(None, ('group', 'expert')), may hold values from -4 to 4
- cache_kv: bfloat16 [2, 256, 2, 128, 2048], P(None, ('group', 'expert')), may hold values from -6 to 6
- seg_len: int32 [256, 2], P(('group', 'expert')), may hold values from 0 to 128, as said below
- o_rows: bfloat16 [2048, 2048], P('expert'), may hold values from -0.125 to 0.125
- norm_gain: float32 [2048], replicated, may hold values from 0.25 to 1.75
- routes: int32 [32768, 8], P(('group', 'expert')), may hold values from 0 to 31, all different within a row; in each aligned block of 128 rows (0 to 127, 128 to 255, ...) at most 48 rows name the same one
- route_wts: float32 [32768, 8], P(('group', 'expert')), may hold values from 0.05 to 0.6
- w_in: bfloat16 [32, 2048, 1024], P('expert'), may hold values from -0.125 to 0.125
- w_out: bfloat16 [32, 512, 2048], P('expert'), may hold values from -0.25 to 0.25
Outputs:
- layer_out: bfloat16 [32768, 2048], P(('group', 'expert'))
Inputs may be any that keep to these rules, and one draw needn't show every extreme that they name: seg_len[d, 0] is 1 to 128; seg_len[d, 1] is 0 (the paired request is short) or 1 to 128; seg_len[0, 0] and seg_len[0, 1] are 128 and seg_len[1, 1] is 0. `routes`: each row names 8 different experts; among the 128 rows of one device no expert is named more than 48 times.
All inputs are finite; a program needn't handle non-finite values.
Results may differ from a plain program's by a relative error of at most 0.0053.
Values may be sent and summed in bfloat16 or wider, within the bound.
A program may use at most 128 MiB of HBM per device.

v0:
```python
import math
import jax
import jax.numpy as jnp
from jax import lax
from jax.sharding import PartitionSpec as P

HEADS = 16
HD = 128
FF = 512
TOPK = 8


def swapped(block, axis, distance):
    count = lax.axis_size(axis)
    route = []
    for low in range(count):
        high = low | 1 << distance
        if high != low and high < count:
            route += [(low, high), (high, low)]
    return lax.ppermute(block, axis, route)


def attend(query_rows, key_rows, value_rows, valid_keys):
    q_heads = query_rows.reshape(query_rows.shape[0], HEADS, HD)
    k_heads = key_rows.reshape(key_rows.shape[0], HEADS, HD)
    v_heads = value_rows.reshape(value_rows.shape[0], HEADS, HD)
    scores = jnp.einsum("chd,shd->hcs", q_heads, k_heads, preferred_element_type=jnp.float32) * (
        1.0 / math.sqrt(HD)
    )
    scores = jnp.where(valid_keys[None, None, :], scores, -1e30)
    peak_score = jnp.max(scores, axis=-1)
    expo = jnp.where(valid_keys[None, None, :], jnp.exp(scores - peak_score[..., None]), 0.0)
    totals = jnp.sum(expo, axis=-1)
    probs_low = expo.astype(jnp.bfloat16)
    accum_out = jnp.einsum("hcs,shd->chd", probs_low, v_heads, preferred_element_type=jnp.float32)
    return (peak_score, totals, accum_out)


def merge_parts(first, second):
    peak_a, total_a, accum_a = first
    peak_b, total_b, accum_b = second
    peak_both = jnp.maximum(peak_a, peak_b)
    scale_a = jnp.exp(peak_a - peak_both).T
    scale_b = jnp.exp(peak_b - peak_both).T
    numer = accum_a * scale_a[:, :, None] + accum_b * scale_b[:, :, None]
    denom = total_a.T * scale_a + total_b.T * scale_b
    merged = numer / denom[:, :, None]
    return merged.reshape(merged.shape[0], -1).astype(jnp.bfloat16)


def expert_mlp(token_rows, weight_in, weight_out):
    joined = jnp.dot(token_rows, weight_in, preferred_element_type=jnp.float32)
    hidden = (jax.nn.silu(joined[:, :FF]) * joined[:, FF:]).astype(jnp.bfloat16)
    return jnp.dot(hidden, weight_out, preferred_element_type=jnp.float32).astype(jnp.bfloat16)


def shards(
    resid, queries, span_kv, cache_kv, seg_len, o_rows, norm_gain, routes, route_wts, w_in, w_out
):
    span_rows = queries.shape[0]
    seg_rows = cache_kv.shape[3]
    width = queries.shape[1]
    experts_here = lax.axis_size("expert")
    positions = jnp.arange(seg_rows, dtype=jnp.int32)
    keys_a = jnp.concatenate([span_kv[0], cache_kv[0, 0, 0]], axis=0)
    vals_a = jnp.concatenate([span_kv[1], cache_kv[1, 0, 0]], axis=0)
    valid_a = jnp.concatenate([jnp.ones((span_rows,), bool), positions < seg_len[0, 0]])
    part_a = attend(queries, keys_a, vals_a, valid_a)
    length_low = seg_len[0, 1:2].astype(jnp.float32).astype(jnp.bfloat16)
    fetched, fetched_len = swapped((cache_kv[:, 0, 1], length_low), "group", 0)
    valid_b = positions.astype(jnp.float32) < fetched_len[0].astype(jnp.float32)
    part_b = attend(queries, fetched[0], fetched[1], valid_b)
    attended = merge_parts(part_a, part_b)
    projected = jnp.dot(
        attended,
        lax.all_gather(o_rows, "expert", axis=0, tiled=True),
        preferred_element_type=jnp.float32,
    )
    residual = resid.astype(jnp.float32) + projected
    normed = (
        residual
        * lax.rsqrt(jnp.mean(residual * residual, axis=-1, keepdims=True) + 1e-05)
        * norm_gain
    ).astype(jnp.bfloat16)
    capacity = min(span_rows, span_rows * TOPK * 3 // (2 * experts_here))
    onehot = (
        routes[:, :, None] == jnp.arange(experts_here, dtype=jnp.int32)[None, None, :]
    ).astype(jnp.int32)
    counts = jnp.sum(onehot, axis=1)
    before = jnp.cumsum(counts, axis=0) - counts
    slot_ids = jnp.sum(onehot * before[:, None, :], axis=-1)
    flat_slot = routes * capacity + slot_ids
    placing = jnp.any(
        flat_slot[None, :, :]
        == jnp.arange(experts_here * capacity, dtype=jnp.int32)[:, None, None],
        axis=-1,
    )
    outgoing = jnp.dot(
        placing.astype(jnp.bfloat16), normed, preferred_element_type=jnp.float32
    ).astype(jnp.bfloat16)
    outgoing = outgoing.reshape(experts_here, capacity, width)
    arrived = lax.all_to_all(outgoing, "expert", split_axis=0, concat_axis=0, tiled=True)
    flat_rows = arrived.reshape(-1, width)
    output_rows = expert_mlp(flat_rows, w_in[0], w_out[0]).reshape(arrived.shape)
    returned_rows = lax.all_to_all(output_rows, "expert", split_axis=0, concat_axis=0, tiled=True)
    returned_rows = returned_rows.reshape(experts_here * capacity, width)
    expert_sum = jnp.zeros((span_rows, width), jnp.float32)
    for route_k in range(TOPK):
        picked = returned_rows[flat_slot[:, route_k]].astype(jnp.float32)
        expert_sum = expert_sum + route_wts[:, route_k, None] * picked
    return (residual + expert_sum).astype(jnp.bfloat16)


def solution(mesh):
    placed = (
        P(("group", "expert"), None),
        P(("group", "expert"), None),
        P(None, ("group", "expert"), None),
        P(None, ("group", "expert"), None, None, None),
        P(("group", "expert"), None),
        P("expert", None),
        P(),
        P(("group", "expert"), None),
        P(("group", "expert"), None),
        P("expert", None, None),
        P("expert", None, None),
    )
    return jax.shard_map(
        shards, mesh=mesh, in_specs=placed, out_specs=P(("group", "expert"), None), check_vma=False
    )
```

profile of v0, /device:TPU:33, one launch (start us, length us, event | category | flops | bytes accessed | tf_op | source)
XLA Modules:
  0.0 479.4 jit_solution(5816244615594503621)
XLA Ops:
  6.5 0.0 copy-start
  6.5 0.0 all-gather.2.cloned.1.call-start
  6.5 0.7 all-gather.2.cloned.1.call-update
  7.3 1.3 fusion.66
  9.2 1.6 collective-permute-start
  10.8 1.3 slice.87
  12.1 1.3 copy.55
  13.4 0.0 collective-permute-start.1
  13.4 2.1 fusion.65
  15.5 1.3 copy.53
  16.8 1.1 copy.39
  17.9 0.0 copy-start.6
  17.9 2.3 fusion.63
  20.2 1.3 copy.54
  21.5 1.1 copy.40
  22.6 1.0 copy.35
  23.6 2.1 copy.36
  25.7 0.0 copy-done.6
  25.7 0.1 copy.47
  25.8 0.2 reduce_window_sum.11
  26.0 0.1 copy.49
  26.1 0.6 iota_compare_fusion.2
  26.8 5.6 %fusion = pred[1536,128]{1,0:T(8,128)(4,1)S(1)} fusion(s32[128,8]{0,1:T(8,128)S(1)} %multiply_add_fusion), kind=kLoop, calls=%fused_computation.11 | loop fusion | flops 2949120 | bytes 200704 | tf_op jit(solution)/shard_map/reduce_or | solution.py:93
  32.4 1.9 bitcast_reduce_fusion
  34.2 0.0 copy-start.1
  34.2 0.0 copy-start.3
  34.2 1.3 copy-done.1
  35.6 0.6 fusion.9
  36.2 0.0 copy-start.4
  36.2 0.0 collective-permute-done
  36.9 0.0 copy-start.2
  36.9 0.0 copy-start.5
  37.0 0.0 collective-permute-done.1
  37.0 1.4 fusion.64
  38.4 0.0 copy-done.3
  38.4 0.5 fusion.67
  39.0 0.2 fusion.31
  39.2 0.0 copy-done.4
  39.2 0.0 copy-done.2
  39.2 0.0 copy-done.5
  39.2 0.8 fusion.14
  40.0 1.2 fusion.16
  41.2 67.1 %all-gather.2.cloned.1.call-done = bf16[2048,2048]{1,0:T(8,128)(2,1)} async-done(((bf16[64,2048]{1,0:T(8,128)(2,1)}), bf16[2048,2048]{1,0:T(8,128)(2,1)}) %all-gather.2.cloned.1.call-update) | async-done | bytes 8388624 | tf_op jit(solution)/shard_map/all_gather | solution.py:76
  108.3 4.9 %multiply_reduce_fusion = (f32[128]{0:T(128)S(1)}, f32[128,2048]{1,0:T(8,128)S(1)}) fusion(bf16[128,2048]{0,1:T(8,128)(2,1)} %bitcast.126, bf16[2048,2048]{1,0:T(8,128)(2,1)} %all-gather.2.cloned.1.call-done, bf16[128,2048]{1,0:T(8,128)(2,1)} %param.11), kind=kOutput, calls=%fused_computation.44 | convolution fusion | flops 1074790272 | bytes 10486272 | tf_op jit(solution)/shard_map/dot_general | solution.py:74
  113.2 0.0 copy-done.7
  113.2 1.9 convolution_convert_fusion.1
  115.1 0.0 copy-start.9
  115.1 145.8 %all_to_all.10 = bf16[32,48,2048]{2,1,0:T(8,128)(2,1)S(1)} all-to-all(bf16[32,48,2048]{2,1,0:T(8,128)(2,1)S(1)} %bitcast.120), channel_id=1, replica_groups=mesh['group'=8,'expert'=32] {'expert'}, dimensions={0} | all-to-all | bytes 12582912 | tf_op jit(solution)/shard_map/all_to_all | solution.py:102
  260.9 0.0 copy-done.9
  260.9 6.8 %fusion.1 = f32[1536,1024]{1,0:T(8,128)S(1)} fusion(bf16[1536,2048]{1,0:T(8,128)(2,1)S(1)} %bitcast.122, bf16[1,2048,1024]{2,1,0:T(8,128)(2,1)S(1)} %copy-done.9), kind=kOutput, calls=%fused_computation.12 | convolution fusion | flops 6442450944 | bytes 16777216 | tf_op jit(solution)/shard_map/dot_general | solution.py:52
  267.7 0.0 copy-done
  267.7 5.4 %convolution_convert_fusion = bf16[1536,2048]{1,0:T(8,128)(2,1)} fusion(bf16[1,512,2048]{2,1,0:T(8,128)(2,1)S(1)} %copy-done, f32[1536,1024]{1,0:T(8,128)S(1)} %fusion.1), kind=kOutput, calls=%fused_computation.8 | convolution fusion | flops 3229089792 | bytes 14680064 | tf_op jit(solution)/shard_map/dot_general | solution.py:54
  273.1 7.4 %all-to-all-start.1 = ((bf16[32,48,2048]{2,1,0:T(8,128)(2,1)}), bf16[32,48,2048]{2,1,0:T(8,128)(2,1)}, u32[]{:S(2)}, u32[]{:S(2)}) async-start(bf16[32,48,2048]{2,1,0:T(8,128)(2,1)} %bitcast.121), calls=%async_computation.1 | async-start | bytes 12582912 | tf_op jit(solution)/shard_map/all_to_all | solution.py:105
  280.5 0.0 copy-done.8
  280.6 140.9 %all-to-all-done.1 = bf16[32,48,2048]{2,1,0:T(8,128)(2,1)} async-done(((bf16[32,48,2048]{2,1,0:T(8,128)(2,1)}), bf16[32,48,2048]{2,1,0:T(8,128)(2,1)}, u32[]{:S(2)}, u32[]{:S(2)}) %all-to-all-start.1) | async-done | bytes 6291488 | tf_op jit(solution)/shard_map/all_to_all | solution.py:105
  421.5 5.8 %gather_fusion = bf16[128,2048]{1,0:T(8,128)(2,1)} fusion(bf16[1536,2048]{1,0:T(8,128)(2,1)} %bitcast.24, s32[1024]{0:T(1024)S(1)} %get-tuple-element.45), kind=kCustom, calls=%fused_computation | custom fusion | bytes 1049088 | tf_op jit(solution)/shard_map/gather | solution.py:109
  427.3 5.9 %gather_fusion.1 = bf16[128,2048]{1,0:T(8,128)(2,1)} fusion(bf16[1536,2048]{1,0:T(8,128)(2,1)} %bitcast.24, s32[1024]{0:T(1024)S(1)} %get-tuple-element.44), kind=kCustom, calls=%fused_computation.1 | custom fusion | bytes 1049088 | tf_op jit(solution)/shard_map/gather | solution.py:109
  433.2 5.9 %gather_fusion.2 = bf16[128,2048]{1,0:T(8,128)(2,1)} fusion(bf16[1536,2048]{1,0:T(8,128)(2,1)} %bitcast.24, s32[1024]{0:T(1024)S(1)} %get-tuple-element.43), kind=kCustom, calls=%fused_computation.2 | custom fusion | bytes 1049088 | tf_op jit(solution)/shard_map/gather | solution.py:109
  439.1 5.9 %gather_fusion.3 = bf16[128,2048]{1,0:T(8,128)(2,1)} fusion(bf16[1536,2048]{1,0:T(8,128)(2,1)} %bitcast.24, s32[1024]{0:T(1024)S(1)} %get-tuple-element.42), kind=kCustom, calls=%fused_computation.3 | custom fusion | bytes 1049088 | tf_op jit(solution)/shard_map/gather | solution.py:109
  444.9 5.8 %gather_fusion.4 = bf16[128,2048]{1,0:T(8,128)(2,1)} fusion(bf16[1536,2048]{1,0:T(8,128)(2,1)} %bitcast.24, s32[1024]{0:T(1024)S(1)} %get-tuple-element.41), kind=kCustom, calls=%fused_computation.4 | custom fusion | bytes 1049088 | tf_op jit(solution)/shard_map/gather | solution.py:109
  450.7 5.8 %gather_fusion.5 = bf16[128,2048]{1,0:T(8,128)(2,1)} fusion(bf16[1536,2048]{1,0:T(8,128)(2,1)} %bitcast.24, s32[1024]{0:T(1024)S(1)} %get-tuple-element.40), kind=kCustom, calls=%fused_computation.5 | custom fusion | bytes 1049088 | tf_op jit(solution)/shard_map/gather | solution.py:109
  456.6 6.1 %gather_fusion.6 = bf16[128,2048]{1,0:T(8,128)(2,1)} fusion(bf16[1536,2048]{1,0:T(8,128)(2,1)} %bitcast.24, s32[1024]{0:T(1024)S(1)} %get-tuple-element.39), kind=kCustom, calls=%fused_computation.6 | custom fusion | bytes 1049088 | tf_op jit(solution)/shard_map/gather | solution.py:109
  462.6 5.8 %gather_fusion.7 = bf16[128,2048]{1,0:T(8,128)(2,1)} fusion(bf16[1536,2048]{1,0:T(8,128)(2,1)} %bitcast.24, s32[1024]{0:T(1024)S(1)} %get-tuple-element.38), kind=kCustom, calls=%fused_computation.7 | custom fusion | bytes 1049088 | tf_op jit(solution)/shard_map/gather | solution.py:109
  468.5 3.9 add_convert_fusion
  (16 shorter events, 0.1 us)
Async XLA Ops:
  6.5 261.2 %copy-start = (bf16[1,512,2048]{2,1,0:T(8,128)(2,1)S(1)}, bf16[1,512,2048]{2,1,0:T(8,128)(2,1)}, u32[]{:S(2)}) copy-start(bf16[1,512,2048]{2,1,0:T(8,128)(2,1)} %param.21) | copy-start | bytes 6291460
  6.5 101.7 %all-gather.2.cloned.1.call-start = ((), (), s32[]{:S(2)}) async-start(), calls=%async_computation.2 | async-start | bytes 8650752 | tf_op jit(solution)/shard_map/all_gather | solution.py:76
  9.2 27.0 %collective-permute-start = (bf16[1]{0:T(256)(128)(2,1)}, bf16[1]{0:T(256)(128)(2,1)}, u32[]{:S(2)}, u32[]{:S(2)}) collective-permute-start(bf16[1]{0:T(256)(128)(2,1)} %bitcast.8), channel_id=1, source_target_pairs={{0,32},{32,0},{64,96},{96,64},{128,160},{160,128},{192,224},{224,1... | collective-permute-start | bytes 14 | tf_op jit(solution)/shard_map/ppermute | solution.py:20
  13.4 23.5 %collective-permute-start.1 = (bf16[2,128,2048]{1,2,0:T(8,128)(2,1)}, bf16[2,128,2048]{1,2,0:T(8,128)(2,1)}, u32[]{:S(2)}, u32[]{:S(2)}) collective-permute-start(bf16[2,128,2048]{1,2,0:T(8,128)(2,1)} %bitcast.127), channel_id=1, source_target_pairs={{0,32},{32,0},{64,96},{96,64},{128,160},{160,128},{192,224},{224,1... | collective-permute-start | bytes 3145736 | tf_op jit(solution)/shard_map/ppermute | solution.py:20
  17.9 7.8 %copy-start.6 = (s32[128,8]{0,1:T(8,128)S(1)}, s32[128,8]{0,1:T(8,128)}, u32[]{:S(2)}) copy-start(s32[128,8]{0,1:T(8,128)} %param.18) | copy-start | bytes 12292
  34.2 1.4 copy-start.1
  34.2 4.2 copy-start.3
  36.2 3.0 copy-start.4
  36.9 2.3 copy-start.2
  36.9 2.3 copy-start.5
  108.3 5.0 %copy-start.7 = (f32[2048]{0:T(1024)S(1)}, f32[2048]{0:T(1024)}, u32[]{:S(2)}) copy-start(f32[2048]{0:T(1024)} %param.17) | copy-start | bytes 24580
  115.1 145.8 %copy-start.9 = (bf16[1,2048,1024]{2,1,0:T(8,128)(2,1)S(1)}, bf16[1,2048,1024]{2,1,0:T(8,128)(2,1)}, u32[]{:S(2)}) copy-start(bf16[1,2048,1024]{2,1,0:T(8,128)(2,1)} %param.20) | copy-start | bytes 12582916
  273.1 7.4 %copy-start.8 = (f32[128,8]{0,1:T(8,128)S(1)}, f32[128,8]{0,1:T(8,128)}, u32[]{:S(2)}) copy-start(f32[128,8]{0,1:T(8,128)} %param.19) | copy-start | bytes 12292
  273.1 148.4 %all-to-all-start.1 = ((bf16[32,48,2048]{2,1,0:T(8,128)(2,1)}), bf16[32,48,2048]{2,1,0:T(8,128)(2,1)}, u32[]{:S(2)}, u32[]{:S(2)}) async-start(bf16[32,48,2048]{2,1,0:T(8,128)(2,1)} %bitcast.121), calls=%async_computation.1 | async-start | bytes 12582912 | tf_op jit(solution)/shard_map/all_to_all | solution.py:105
Sparse Core Ops, SparseCore 0:
  9.9 98.2 all-gather.1
where the time goes:
time: 489 us; the launch traced here: 479 us
  waiting for transfers between devices  209 us (43%)
  blocking collectives  146 us (30%)
  local copies, waits for them, and re-layouts  66.1 us (14%)
  matrix products  23.3 us (5%)
  between operations  15.3 us (3%)
  other arithmetic  11.2 us (2%)
  starting transfers between devices  8.94 us (2%)
    all_to_all x1, blocking collectives, shards(): lax.all_to_all(outgoing, 'expert', split_axis=0, concat_axis=0, tiled=True)  146 us
    all_to_all x1, waiting for transfers between devices, shards(): lax.all_to_all(output_rows, 'expert', split_axis=0, concat_axis=0, tiled=...  141 us
    all_gather x1, waiting for transfers between devices, shards(): lax.all_gather(o_rows, 'expert', axis=0, tiled=True)  67.1 us
    gather x8, local copies, waits for them, and re-layouts, shards(): picked = returned_rows[flat_slot[:, route_k]].astype(jnp.float32)  47 us
  transfers between devices with their start and end apart: 4, of which 2 were waited for; matrix products, arithmetic and copies ran while one was open for 6% of the time, Pallas kernels for 0%

commit v1 on v0

--- a/solution.py
+++ b/solution.py
@@ -8,6 +8,17 @@
 HD = 128
 FF = 512
 TOPK = 8
+
+
+def reach_the_area(work_x, across="expert"):
+    p_count = lax.psum(1, across)
+    return lax.all_to_all(
+        jnp.tile(work_x, tuple((p_count if i0 == 0 else 1 for i0 in range(work_x.ndim)))),
+        across,
+        split_axis=0,
+        concat_axis=0,
+        tiled=True,
+    )
 
 
 def swapped(block, axis, distance):
@@ -71,11 +82,7 @@
     valid_b = positions.astype(jnp.float32) < fetched_len[0].astype(jnp.float32)
     part_b = attend(queries, fetched[0], fetched[1], valid_b)
     attended = merge_parts(part_a, part_b)
-    projected = jnp.dot(
-        attended,
-        lax.all_gather(o_rows, "expert", axis=0, tiled=True),
-        preferred_element_type=jnp.float32,
-    )
+    projected = jnp.dot(attended, reach_the_area(o_rows), preferred_element_type=jnp.float32)
     residual = resid.astype(jnp.float32) + projected
     normed = (
         residual

time: 489 us -> 576 us (1.18); the launches traced: 479 us -> 573 us
  waiting for transfers between devices: 209 us -> 298 us
  between operations: 15.3 us -> 1.98 us
  starting transfers between devices: 8.94 us -> 20.1 us
    all_to_all x0 -> x1, waiting for transfers between devices: none -> 158 us  [reach_the_area(): lax.all_to_all(jnp.tile(work_x, tuple((p_count if i0 == 0 else 1 for i0 i...]
    all_gather x1 -> x0, waiting for transfers between devices: 67.1 us -> none  [shards(): lax.all_gather(o_rows, 'expert', axis=0, tiled=True)]
    all_to_all x0 -> x1, starting transfers between devices: none -> 11 us  [reach_the_area(): lax.all_to_all(jnp.tile(work_x, tuple((p_count if i0 == 0 else 1 for i0 i...]
  transfers between devices with their start and end apart: 4 -> 4, of which waited for: 2 -> 2; matrix products, arithmetic and copies ran while one was open for 6% -> 5% of each run, Pallas kernels for 0% -> 0%
where the time goes in v1:
time: 576 us; the launch traced here: 573 us
  waiting for transfers between devices  298 us (52%)
  blocking collectives  148 us (26%)
  local copies, waits for them, and re-layouts  69.3 us (12%)
  matrix products  23.4 us (4%)
  starting transfers between devices  20.1 us (3%)
  other arithmetic  11.2 us (2%)
    all_to_all x1, waiting for transfers between devices, reach_the_area(): lax.all_to_all(jnp.tile(work_x, tuple((p_count if i0 == 0 else 1 for i0 i...  158 us
    all_to_all x1, blocking collectives, shards(): lax.all_to_all(outgoing, 'expert', split_axis=0, concat_axis=0, tiled=True)  148 us
    all_to_all x1, waiting for transfers between devices, shards(): lax.all_to_all(output_rows, 'expert', split_axis=0, concat_axis=0, tiled=...  141 us
    gather x8, local copies, waits for them, and re-layouts, shards(): picked = returned_rows[flat_slot[:, route_k]].astype(jnp.float32)  47 us
  transfers between devices with their start and end apart: 4, of which 2 were waited for; matrix products, arithmetic and copies ran while one was open for 5% of the time, Pallas kernels for 0%

profile of v1, /device:TPU:33, one launch (start us, length us, event | category | flops | bytes accessed | tf_op | source)
XLA Modules:
  0.0 572.7 jit_solution(9070720545504948641)
XLA Ops:
  0.0 0.0 copy-start
  0.0 5.4 tile.2
  5.4 0.0 slice-start
  5.4 11.0 %all-to-all-start = ((bf16[32,64,2048]{2,1,0:T(8,128)(2,1)}), bf16[32,64,2048]{2,1,0:T(8,128)(2,1)}, u32[]{:S(2)}, u32[]{:S(2)}) async-start(bf16[32,64,2048]{2,1,0:T(8,128)(2,1)} %tile.2), calls=%async_computation | async-start | bytes 16777216 | tf_op jit(solution)/shard_map/all_to_all | solution.py:15
  16.4 0.0 copy-done.9
  16.4 0.6 fusion.66
  17.6 2.1 collective-permute-start
  19.8 0.0 slice-done
  19.8 1.3 copy.55
  21.1 0.3 collective-permute-start.1
  21.4 2.1 fusion.65
  23.5 1.3 copy.53
  24.8 1.0 copy.39
  25.8 2.3 fusion.63
  28.1 1.3 copy.54
  29.4 1.0 copy.40
  30.4 1.0 copy.35
  31.4 2.0 copy.36
  33.5 0.0 copy-done.6
  33.5 0.1 copy.47
  33.6 0.2 reduce_window_sum.11
  33.8 0.1 copy.49
  33.8 0.6 iota_compare_fusion.2
  34.6 5.6 fusion
  40.1 1.8 bitcast_reduce_fusion
  42.0 0.0 copy-start.1
  42.0 0.0 copy-start.3
  42.0 1.3 copy-done.1
  43.3 0.6 fusion.9
  44.0 0.0 copy-start.4
  44.8 0.0 copy-start.2
  44.8 0.0 copy-start.5
  44.8 0.0 collective-permute-done.1
  44.8 1.4 fusion.64
  46.2 0.0 copy-done.3
  46.2 0.5 fusion.67
  46.8 0.2 fusion.31
  47.0 0.0 copy-done.4
  47.0 0.0 copy-done.2
  47.1 0.0 copy-done.5
  47.1 0.8 fusion.14
  47.8 1.2 fusion.16
  49.0 157.6 %all-to-all-done = bf16[32,64,2048]{2,1,0:T(8,128)(2,1)} async-done(((bf16[32,64,2048]{2,1,0:T(8,128)(2,1)}), bf16[32,64,2048]{2,1,0:T(8,128)(2,1)}, u32[]{:S(2)}, u32[]{:S(2)}) %all-to-all-start) | async-done | bytes 8388640 | tf_op jit(solution)/shard_map/all_to_all | solution.py:15
  206.6 4.9 multiply_reduce_fusion
  211.5 0.0 copy-done.7
  211.6 1.9 convolution_convert_fusion.1
  213.4 0.0 copy-start.10
  213.4 148.4 %all_to_all.19 = bf16[32,48,2048]{2,1,0:T(8,128)(2,1)S(1)} all-to-all(bf16[32,48,2048]{2,1,0:T(8,128)(2,1)S(1)} %bitcast.121), channel_id=1, replica_groups=mesh['group'=8,'expert'=32] {'expert'}, dimensions={0} | all-to-all | bytes 12582912 | tf_op jit(solution)/shard_map/all_to_all | solution.py:109
  361.9 0.0 copy-done.10
  361.9 6.8 %fusion.1 = f32[1536,1024]{1,0:T(8,128)S(1)} fusion(bf16[1536,2048]{1,0:T(8,128)(2,1)S(1)} %bitcast.123, bf16[1,2048,1024]{2,1,0:T(8,128)(2,1)S(1)} %copy-done.10), kind=kOutput, calls=%fused_computation.12 | convolution fusion | flops 6442450944 | bytes 16777216 | tf_op jit(solution)/shard_map/dot_general | solution.py:63
  368.7 0.0 copy-done
  368.7 5.4 convolution_convert_fusion
  374.1 6.7 %all-to-all-start.2 = ((bf16[32,48,2048]{2,1,0:T(8,128)(2,1)}), bf16[32,48,2048]{2,1,0:T(8,128)(2,1)}, u32[]{:S(2)}, u32[]{:S(2)}) async-start(bf16[32,48,2048]{2,1,0:T(8,128)(2,1)} %bitcast.122), calls=%async_computation.2 | async-start | bytes 12582912 | tf_op jit(solution)/shard_map/all_to_all | solution.py:112
  380.9 0.0 copy-done.8
  380.9 140.7 %all-to-all-done.2 = bf16[32,48,2048]{2,1,0:T(8,128)(2,1)} async-done(((bf16[32,48,2048]{2,1,0:T(8,128)(2,1)}), bf16[32,48,2048]{2,1,0:T(8,128)(2,1)}, u32[]{:S(2)}, u32[]{:S(2)}) %all-to-all-start.2) | async-done | bytes 6291488 | tf_op jit(solution)/shard_map/all_to_all | solution.py:112
  521.6 5.8 %gather_fusion = bf16[128,2048]{1,0:T(8,128)(2,1)} fusion(bf16[1536,2048]{1,0:T(8,128)(2,1)} %bitcast.25, s32[1024]{0:T(1024)S(1)} %get-tuple-element.45), kind=kCustom, calls=%fused_computation | custom fusion | bytes 1049088 | tf_op jit(solution)/shard_map/gather | solution.py:116
  527.4 5.9 %gather_fusion.1 = bf16[128,2048]{1,0:T(8,128)(2,1)} fusion(bf16[1536,2048]{1,0:T(8,128)(2,1)} %bitcast.25, s32[1024]{0:T(1024)S(1)} %get-tuple-element.44), kind=kCustom, calls=%fused_computation.1 | custom fusion | bytes 1049088 | tf_op jit(solution)/shard_map/gather | solution.py:116
  533.3 5.9 %gather_fusion.2 = bf16[128,2048]{1,0:T(8,128)(2,1)} fusion(bf16[1536,2048]{1,0:T(8,128)(2,1)} %bitcast.25, s32[1024]{0:T(1024)S(1)} %get-tuple-element.43), kind=kCustom, calls=%fused_computation.2 | custom fusion | bytes 1049088 | tf_op jit(solution)/shard_map/gather | solution.py:116
  539.2 5.9 %gather_fusion.3 = bf16[128,2048]{1,0:T(8,128)(2,1)} fusion(bf16[1536,2048]{1,0:T(8,128)(2,1)} %bitcast.25, s32[1024]{0:T(1024)S(1)} %get-tuple-element.42), kind=kCustom, calls=%fused_computation.3 | custom fusion | bytes 1049088 | tf_op jit(solution)/shard_map/gather | solution.py:116
  545.0 5.8 %gather_fusion.4 = bf16[128,2048]{1,0:T(8,128)(2,1)} fusion(bf16[1536,2048]{1,0:T(8,128)(2,1)} %bitcast.25, s32[1024]{0:T(1024)S(1)} %get-tuple-element.41), kind=kCustom, calls=%fused_computation.4 | custom fusion | bytes 1049088 | tf_op jit(solution)/shard_map/gather | solution.py:116
  550.8 5.8 %gather_fusion.5 = bf16[128,2048]{1,0:T(8,128)(2,1)} fusion(bf16[1536,2048]{1,0:T(8,128)(2,1)} %bitcast.25, s32[1024]{0:T(1024)S(1)} %get-tuple-element.40), kind=kCustom, calls=%fused_computation.5 | custom fusion | bytes 1049088 | tf_op jit(solution)/shard_map/gather | solution.py:116
  556.7 6.1 %gather_fusion.6 = bf16[128,2048]{1,0:T(8,128)(2,1)} fusion(bf16[1536,2048]{1,0:T(8,128)(2,1)} %bitcast.25, s32[1024]{0:T(1024)S(1)} %get-tuple-element.39), kind=kCustom, calls=%fused_computation.6 | custom fusion | bytes 1049088 | tf_op jit(solution)/shard_map/gather | solution.py:116
  562.8 5.8 %gather_fusion.7 = bf16[128,2048]{1,0:T(8,128)(2,1)} fusion(bf16[1536,2048]{1,0:T(8,128)(2,1)} %bitcast.25, s32[1024]{0:T(1024)S(1)} %get-tuple-element.38), kind=kCustom, calls=%fused_computation.7 | custom fusion | bytes 1049088 | tf_op jit(solution)/shard_map/gather | solution.py:116
  568.6 3.9 add_convert_fusion
  (19 shorter events, 0.2 us)
Async XLA Ops:
  0.0 368.7 %copy-start = (bf16[1,512,2048]{2,1,0:T(8,128)(2,1)S(1)}, bf16[1,512,2048]{2,1,0:T(8,128)(2,1)}, u32[]{:S(2)}) copy-start(bf16[1,512,2048]{2,1,0:T(8,128)(2,1)} %param.21) | copy-start | bytes 6291460
  5.4 11.0 %copy-start.9 = (s32[1,2]{1,0:T(1,128)S(1)}, s32[1,2]{1,0:T(1,128)}, u32[]{:S(2)}) copy-start(s32[1,2]{1,0:T(1,128)} %param.15) | copy-start | bytes 28
  5.4 14.4 %slice-start = ((bf16[2,1,2,128,2048]{4,3,2,1,0:T(8,128)(2,1)}), bf16[2,1,1,128,2048]{4,3,2,1,0:T(8,128)(2,1)S(1)}, s32[]{:S(2)}) async-start(bf16[2,1,2,128,2048]{4,3,2,1,0:T(8,128)(2,1)} %param.14), calls=%async_computation.3 | async-start | bytes 2097152 | tf_op jit(solution)/shard_map/slice | solution.py:81
  5.4 201.2 %all-to-all-start = ((bf16[32,64,2048]{2,1,0:T(8,128)(2,1)}), bf16[32,64,2048]{2,1,0:T(8,128)(2,1)}, u32[]{:S(2)}, u32[]{:S(2)}) async-start(bf16[32,64,2048]{2,1,0:T(8,128)(2,1)} %tile.2), calls=%async_computation | async-start | bytes 16777216 | tf_op jit(solution)/shard_map/all_to_all | solution.py:15
  17.6 26.4 %collective-permute-start = (bf16[1]{0:T(256)(128)(2,1)}, bf16[1]{0:T(256)(128)(2,1)}, u32[]{:S(2)}, u32[]{:S(2)}) collective-permute-start(bf16[1]{0:T(256)(128)(2,1)} %bitcast.8), channel_id=1, source_target_pairs={{0,32},{32,0},{64,96},{96,64},{128,160},{160,128},{192,224},{224,1... | collective-permute-start | bytes 14 | tf_op jit(solution)/shard_map/ppermute | solution.py:31
  21.1 23.7 %collective-permute-start.1 = (bf16[2,128,2048]{1,2,0:T(8,128)(2,1)}, bf16[2,128,2048]{1,2,0:T(8,128)(2,1)}, u32[]{:S(2)}, u32[]{:S(2)}) collective-permute-start(bf16[2,128,2048]{1,2,0:T(8,128)(2,1)} %bitcast.128), channel_id=1, source_target_pairs={{0,32},{32,0},{64,96},{96,64},{128,160},{160,128},{192,224},{224,1... | collective-permute-start | bytes 3145736 | tf_op jit(solution)/shard_map/ppermute | solution.py:31
  25.8 7.7 %copy-start.6 = (s32[128,8]{0,1:T(8,128)S(1)}, s32[128,8]{0,1:T(8,128)}, u32[]{:S(2)}) copy-start(s32[128,8]{0,1:T(8,128)} %param.18) | copy-start | bytes 12292
  42.0 1.4 copy-start.1
  42.0 4.2 copy-start.3
  44.0 3.0 copy-start.4
  44.8 2.3 copy-start.2
  44.8 2.3 copy-start.5
  206.6 5.0 copy-start.7
  213.4 148.5 %copy-start.10 = (bf16[1,2048,1024]{2,1,0:T(8,128)(2,1)S(1)}, bf16[1,2048,1024]{2,1,0:T(8,128)(2,1)}, u32[]{:S(2)}) copy-start(bf16[1,2048,1024]{2,1,0:T(8,128)(2,1)} %param.20) | copy-start | bytes 12582916
  374.1 6.8 %copy-start.8 = (f32[128,8]{0,1:T(8,128)S(1)}, f32[128,8]{0,1:T(8,128)}, u32[]{:S(2)}) copy-start(f32[128,8]{0,1:T(8,128)} %param.19) | copy-start | bytes 12292
  374.1 147.5 %all-to-all-start.2 = ((bf16[32,48,2048]{2,1,0:T(8,128)(2,1)}), bf16[32,48,2048]{2,1,0:T(8,128)(2,1)}, u32[]{:S(2)}, u32[]{:S(2)}) async-start(bf16[32,48,2048]{2,1,0:T(8,128)(2,1)} %bitcast.122), calls=%async_computation.2 | async-start | bytes 12582912 | tf_op jit(solution)/shard_map/all_to_all | solution.py:112
